TPU v7x, 32 devices: a whole 2x2x4 slice. The times are simulated.
32 devices in a mesh: rep: 8 (over y, x, core), shard: 4 (over z).
Axes of the slice: x: 2, y: 2, z: 4, core: 2. Of those that a mesh axis runs over, the one named last changes fastest.
Arguments:
- tokens: bfloat16 [16, 1024, 768], P('rep', 'shard'), may hold values from -6 to 6
- gain_attn: bfloat16 [768], P('shard'), may hold values from 0.25 to 1.75
- bias_attn: bfloat16 [768], P('shard'), may hold values from -1.5 to 1.5
- w_qkv: bfloat16 [768, 2304], P('shard'), may hold values from -0.21875 to 0.21875
- w_feature: bfloat16 [768, 128], P('shard'), may hold values from -1.5 to 1.5
- w_out: bfloat16 [768, 768], P('shard'), may hold values from -0.875 to 0.875
- gain_mlp: bfloat16 [768], P('shard'), may hold values from 0.25 to 1.75
- bias_mlp: bfloat16 [768], P('shard'), may hold values from -1.5 to 1.5
- w_up: bfloat16 [768, 3072], P('shard'), may hold values from -0.21875 to 0.21875
- w_down: bfloat16 [3072, 768], P('shard'), may hold values from -0.109375 to 0.109375
- cotangent: bfloat16 [16, 1024, 768], P('rep', 'shard'), may hold values from -6 to 6
Outputs:
- block_out: bfloat16 [16, 1024, 768], P('rep', 'shard')
- grad_tokens: bfloat16 [16, 1024, 768], P('rep', 'shard')
- grad_gain_attn: float32 [768], P('shard')
- grad_bias_attn: float32 [768], P('shard')
- grad_w_qkv: float32 [768, 2304], P('shard')
- grad_w_feature: float32 [768, 128], P('shard')
- grad_w_out: float32 [768, 768], P('shard')
- grad_gain_mlp: float32 [768], P('shard')
- grad_bias_mlp: float32 [768], P('shard')
- grad_w_up: float32 [768, 3072], P('shard')
- grad_w_down: float32 [3072, 768], P('shard')
All inputs are finite; a program needn't handle non-finite values.
Results may differ from a plain program's by a relative error of at most 0.019.
Values may be sent and summed in bfloat16 or wider, within the bound.
No kernel may reach another device: no remote copies, remote signals or barrier semaphores. Data moves between devices by JAX's collectives and lax.ppermute only.
A program may use at most 192 MiB of HBM per device.

v0:
```python
import jax
import jax.numpy as jnp
from jax import lax
from jax.sharding import PartitionSpec as P

D = 768
HEADS = 12
HEAD = 64
FEAT = 128
STRETCH = 64
top_precision = lax.Precision.HIGHEST
norm_epsilon = 1e-05


def prefix(value, axis, combine, identity):
    count, here = (lax.axis_size(axis), lax.axis_index(axis))
    everything = jax.tree.map(
        lambda part, kind: lax.all_gather(part.astype(kind), axis),
        value,
        (jnp.bfloat16, jnp.bfloat16),
    )
    start = jax.tree.map(
        lambda part, zero: jnp.broadcast_to(jnp.asarray(zero, part.dtype), part.shape),
        value,
        identity,
    )

    def lap(k, before):
        reached = k < here
        new = combine(
            before, jax.tree.map(lambda part, own: part[k].astype(own.dtype), everything, value)
        )
        return jax.tree.map(lambda a, b: jnp.where(reached, a, b), new, before)

    return lax.fori_loop(0, count, lap, start)


def prefix_2(value, axis, join, neutral):
    count = lax.axis_size(axis)
    place = lax.axis_index(axis)
    ahead = count - 1 - place
    gathered = jax.tree.map(
        lambda a, kind: lax.all_gather(a.astype(kind), axis),
        value,
        jax.tree.map(lambda a: jnp.bfloat16 if a.dtype == jnp.float32 else a.dtype, value),
    )
    state = jax.tree.map(lambda a, e: jnp.zeros_like(a) + jnp.asarray(e, a.dtype), value, neutral)

    def one(lap, state):
        source = count - 1 - lap
        return join(
            state,
            jax.tree.map(
                lambda a, own: lax.dynamic_index_in_dim(a, source, 0, False).astype(own.dtype),
                gathered,
                value,
            ),
        )

    return lax.fori_loop(0, ahead, one, state)


def layer_norm(rows_in, gain, offset):
    centred = rows_in - jnp.mean(rows_in, axis=-1, keepdims=True)
    spread = jnp.mean(centred * centred, axis=-1, keepdims=True)
    return centred * lax.rsqrt(spread + norm_epsilon) * gain + offset


def featurize(inputs):
    return jnp.concatenate(
        [jax.nn.softmax(inputs, axis=-1), jax.nn.softmax(-inputs, axis=-1)], axis=-1
    )


def featurize_pair(u_query, u_key):
    return (featurize(u_query), featurize(u_key))


def gelu_tanh(pre_act):
    return jax.nn.gelu(pre_act, approximate=True)


def add_states(earlier, later):
    return jax.tree.map(jnp.add, earlier, later)


def shifted_sum(terms):
    running = jnp.cumsum(terms, axis=0)
    return jnp.concatenate([jnp.zeros_like(terms[:1]), running[:-1]], axis=0)


def attend_local(query_wide, key_wide, value_wide, prior_state, prior_total):
    length = query_wide.shape[0]
    blocks = length // STRETCH
    block_q = query_wide.reshape(blocks, STRETCH, HEADS, FEAT)
    block_k = key_wide.reshape(blocks, STRETCH, HEADS, FEAT)
    block_v = value_wide.reshape(blocks, STRETCH, HEADS, HEAD)
    state_terms = jnp.einsum("nshf,nshe->nhfe", block_k, block_v, precision=top_precision)
    total_terms = jnp.sum(block_k, axis=1)
    state_before = prior_state[None] + shifted_sum(state_terms)
    total_before = prior_total[None] + shifted_sum(total_terms)
    positions = jnp.arange(STRETCH)
    causal = positions[:, None] >= positions[None, :]
    scores = jnp.where(
        causal, jnp.einsum("nthf,nshf->nhts", block_q, block_k, precision=top_precision), 0.0
    )
    numerator = jnp.einsum("nhts,nshe->nthe", scores, block_v, precision=top_precision)
    numerator = numerator + jnp.einsum(
        "nthf,nhfe->nthe", block_q, state_before, precision=top_precision
    )
    denominator = jnp.transpose(jnp.sum(scores, axis=3), (0, 2, 1))
    denominator = denominator + jnp.einsum(
        "nthf,nhf->nth", block_q, total_before, precision=top_precision
    )
    return (numerator / denominator[..., None]).reshape(length, HEADS, HEAD)


def shards(
    tokens,
    gain_attn,
    bias_attn,
    w_qkv,
    w_feature,
    w_out,
    gain_mlp,
    bias_mlp,
    w_up,
    w_down,
    cotangent,
):
    shard_count = lax.axis_size("shard")
    local_weights = (
        gain_attn,
        bias_attn,
        w_qkv,
        w_feature,
        w_out,
        gain_mlp,
        bias_mlp,
        w_up,
        w_down,
    )
    totals = [
        jnp.zeros((weight.shape[0] * shard_count,) + weight.shape[1:], jnp.float32)
        for weight in local_weights
    ]
    results = []
    input_grads = []
    for batch_index in range(tokens.shape[0]):
        forward_set = (
            lax.all_gather(gain_attn, "shard", axis=0, tiled=True),
            lax.all_gather(bias_attn, "shard", axis=0, tiled=True),
            lax.all_gather(w_qkv, "shard", axis=0, tiled=True),
            lax.all_gather(w_feature, "shard", axis=0, tiled=True),
            lax.all_gather(w_out, "shard", axis=0, tiled=True),
            lax.all_gather(gain_mlp, "shard", axis=0, tiled=True),
            lax.all_gather(bias_mlp, "shard", axis=0, tiled=True),
            lax.all_gather(w_up, "shard", axis=0, tiled=True),
            lax.all_gather(w_down, "shard", axis=0, tiled=True),
        )
        (
            gain_one,
            bias_one,
            qkv_weight,
            feature_weight,
            out_weight,
            gain_two,
            bias_two,
            up_weight,
            down_weight,
        ) = forward_set
        rows_in = tokens[batch_index].astype(jnp.float32)
        length = rows_in.shape[0]
        normed, norm_pull = jax.vjp(
            layer_norm, rows_in, gain_one.astype(jnp.float32), bias_one.astype(jnp.float32)
        )
        normed_low = normed.astype(jnp.bfloat16)
        mixed = jnp.dot(normed_low, qkv_weight, preferred_element_type=jnp.float32).astype(
            jnp.bfloat16
        )
        queries = mixed[:, :D].reshape(length, HEADS, HEAD)
        key_rows = mixed[:, D : 2 * D].reshape(length, HEADS, HEAD)
        values = mixed[:, 2 * D :].reshape(length, HEADS, HEAD)
        feature_maps = feature_weight.reshape(HEADS, HEAD, 2, HEAD)
        u_query = jnp.einsum(
            "thi,hio->tho", queries, feature_maps[:, :, 0], preferred_element_type=jnp.float32
        )
        u_key = jnp.einsum(
            "thi,hio->tho", key_rows, feature_maps[:, :, 1], preferred_element_type=jnp.float32
        )
        (f_query, f_key), feature_pull = jax.vjp(featurize_pair, u_query, u_key)
        query_low = f_query.astype(jnp.bfloat16)
        key_low = f_key.astype(jnp.bfloat16)
        query_wide = query_low.astype(jnp.float32)
        key_wide = key_low.astype(jnp.float32)
        value_wide = values.astype(jnp.float32)
        key_state = jnp.einsum("shf,she->hfe", key_low, values, preferred_element_type=jnp.float32)
        key_sum = jnp.sum(key_wide, axis=0)
        prior = prefix(
            (key_state, key_sum),
            "shard",
            add_states,
            (jnp.zeros_like(key_state), jnp.zeros_like(key_sum)),
        )
        attended, attend_pull = jax.vjp(
            attend_local, query_wide, key_wide, value_wide, prior[0], prior[1]
        )
        attended_low = attended.reshape(length, D).astype(jnp.bfloat16)
        resid = rows_in + jnp.dot(attended_low, out_weight, preferred_element_type=jnp.float32)
        normed_two, norm_two_pull = jax.vjp(
            layer_norm, resid, gain_two.astype(jnp.float32), bias_two.astype(jnp.float32)
        )
        normed_two_low = normed_two.astype(jnp.bfloat16)
        pre_act = jnp.dot(normed_two_low, up_weight, preferred_element_type=jnp.float32)
        hidden, gelu_pull = jax.vjp(gelu_tanh, pre_act)
        hidden_low = hidden.astype(jnp.bfloat16)
        result = resid + jnp.dot(hidden_low, down_weight, preferred_element_type=jnp.float32)
        results.append(result.astype(jnp.bfloat16))
        qkv_back, feature_back, out_back, up_back, down_back = (
            lax.all_gather(w_qkv, "shard", axis=0, tiled=True),
            lax.all_gather(w_feature, "shard", axis=0, tiled=True),
            lax.all_gather(w_out, "shard", axis=0, tiled=True),
            lax.all_gather(w_up, "shard", axis=0, tiled=True),
            lax.all_gather(w_down, "shard", axis=0, tiled=True),
        )
        grad_out = cotangent[batch_index]
        d_down = jnp.dot(hidden_low.T, grad_out, preferred_element_type=jnp.float32)
        d_hidden = jnp.dot(grad_out, down_back.T, preferred_element_type=jnp.float32)
        (d_pre,) = gelu_pull(d_hidden)
        d_pre_low = d_pre.astype(jnp.bfloat16)
        d_up = jnp.dot(normed_two_low.T, d_pre_low, preferred_element_type=jnp.float32)
        d_normed_two = jnp.dot(d_pre_low, up_back.T, preferred_element_type=jnp.float32)
        d_resid_two, d_gain_two, d_bias_two = norm_two_pull(d_normed_two)
        d_resid = grad_out.astype(jnp.float32) + d_resid_two
        d_resid_low = d_resid.astype(jnp.bfloat16)
        d_out = jnp.dot(attended_low.T, d_resid_low, preferred_element_type=jnp.float32)
        d_attended = jnp.dot(d_resid_low, out_back.T, preferred_element_type=jnp.float32).reshape(
            length, HEADS, HEAD
        )
        d_query_f, d_key_f, d_value_f, local_state, local_sum = attend_pull(d_attended)
        later = prefix_2(
            (local_state, local_sum),
            "shard",
            add_states,
            (jnp.zeros_like(local_state), jnp.zeros_like(local_sum)),
        )
        d_key_f = (
            d_key_f
            + jnp.einsum("hfe,she->shf", later[0], value_wide, precision=top_precision)
            + later[1][None]
        )
        d_value_f = d_value_f + jnp.einsum(
            "hfe,shf->she", later[0], key_wide, precision=top_precision
        )
        d_u_query, d_u_key = feature_pull((d_query_f, d_key_f))
        d_uq_low = d_u_query.astype(jnp.bfloat16)
        d_uk_low = d_u_key.astype(jnp.bfloat16)
        back_maps = feature_back.reshape(HEADS, HEAD, 2, HEAD)
        d_queries = jnp.einsum(
            "tho,hio->thi", d_uq_low, back_maps[:, :, 0], preferred_element_type=jnp.float32
        )
        d_keys = jnp.einsum(
            "tho,hio->thi", d_uk_low, back_maps[:, :, 1], preferred_element_type=jnp.float32
        )
        query_map_grad = jnp.einsum(
            "thi,tho->hio", queries, d_uq_low, preferred_element_type=jnp.float32
        )
        key_map_grad = jnp.einsum(
            "thi,tho->hio", key_rows, d_uk_low, preferred_element_type=jnp.float32
        )
        d_maps = jnp.stack([query_map_grad, key_map_grad], axis=2).reshape(D, FEAT)
        d_mixed = jnp.concatenate(
            [d_queries.reshape(length, D), d_keys.reshape(length, D), d_value_f.reshape(length, D)],
            axis=1,
        ).astype(jnp.bfloat16)
        d_qkv = jnp.dot(normed_low.T, d_mixed, preferred_element_type=jnp.float32)
        d_normed = jnp.dot(d_mixed, qkv_back.T, preferred_element_type=jnp.float32)
        d_rows, d_gain_one, d_bias_one = norm_pull(d_normed)
        input_grads.append((d_resid + d_rows).astype(jnp.bfloat16))
        contributions = (
            d_gain_one,
            d_bias_one,
            d_qkv,
            d_maps,
            d_out,
            d_gain_two,
            d_bias_two,
            d_up,
            d_down,
        )
        totals = [total_sum + new_term for total_sum, new_term in zip(totals, contributions)]
    shares = (
        lax.psum_scatter(
            totals[0].astype(jnp.bfloat16), "shard", scatter_dimension=0, tiled=True
        ).astype(jnp.float32),
        lax.psum_scatter(
            totals[1].astype(jnp.bfloat16), "shard", scatter_dimension=0, tiled=True
        ).astype(jnp.float32),
        lax.psum_scatter(
            totals[2].astype(jnp.bfloat16), "shard", scatter_dimension=0, tiled=True
        ).astype(jnp.float32),
        lax.psum_scatter(
            totals[3].astype(jnp.bfloat16), "shard", scatter_dimension=0, tiled=True
        ).astype(jnp.float32),
        lax.psum_scatter(
            totals[4].astype(jnp.bfloat16), "shard", scatter_dimension=0, tiled=True
        ).astype(jnp.float32),
        lax.psum_scatter(
            totals[5].astype(jnp.bfloat16), "shard", scatter_dimension=0, tiled=True
        ).astype(jnp.float32),
        lax.psum_scatter(
            totals[6].astype(jnp.bfloat16), "shard", scatter_dimension=0, tiled=True
        ).astype(jnp.float32),
        lax.psum_scatter(
            totals[7].astype(jnp.bfloat16), "shard", scatter_dimension=0, tiled=True
        ).astype(jnp.float32),
        lax.psum_scatter(
            totals[8].astype(jnp.bfloat16), "shard", scatter_dimension=0, tiled=True
        ).astype(jnp.float32),
    )
    reduced = (
        lax.psum(shares[0].astype(jnp.bfloat16), "rep").astype(jnp.float32),
        lax.psum(shares[1].astype(jnp.bfloat16), "rep").astype(jnp.float32),
        lax.psum(shares[2].astype(jnp.bfloat16), "rep").astype(jnp.float32),
        lax.psum(shares[3].astype(jnp.bfloat16), "rep").astype(jnp.float32),
        lax.psum(shares[4].astype(jnp.bfloat16), "rep").astype(jnp.float32),
        lax.psum(shares[5].astype(jnp.bfloat16), "rep").astype(jnp.float32),
        lax.psum(shares[6].astype(jnp.bfloat16), "rep").astype(jnp.float32),
        lax.psum(shares[7].astype(jnp.bfloat16), "rep").astype(jnp.float32),
        lax.psum(shares[8].astype(jnp.bfloat16), "rep").astype(jnp.float32),
    )
    return (
        jnp.stack(results),
        jnp.stack(input_grads),
        reduced[0],
        reduced[1],
        reduced[2],
        reduced[3],
        reduced[4],
        reduced[5],
        reduced[6],
        reduced[7],
        reduced[8],
    )


def solution(mesh):
    placed = (
        P("rep", "shard", None),
        P("shard"),
        P("shard"),
        P("shard", None),
        P("shard", None),
        P("shard", None),
        P("shard"),
        P("shard"),
        P("shard", None),
        P("shard", None),
        P("rep", "shard", None),
    )
    return jax.shard_map(
        shards,
        mesh=mesh,
        in_specs=placed,
        out_specs=(
            P("rep", "shard", None),
            P("rep", "shard", None),
            P("shard"),
            P("shard"),
            P("shard", None),
            P("shard", None),
            P("shard", None),
            P("shard"),
            P("shard"),
            P("shard", None),
            P("shard", None),
        ),
        check_vma=False,
    )
```

profile of v0, /device:TPU:0, one launch (start us, length us, event | category | flops | bytes accessed | tf_op | source)
XLA Modules:
  0.0 919.0 jit_solution(16887876758495918346)
XLA Ops:
  14.7 14.5 %all-reduce.15 = (bf16[768]{0:T(1024)(128)(2,1)S(1)}, bf16[768]{0:T(1024)(128)(2,1)S(1)}, bf16[768]{0:T(1024)(128)(2,1)}, bf16[768]{0:T(1024)(128)(2,1)}) all-reduce(bf16[768]{0:T(1024)(128)(2,1)S(1)} %dynamic-update-slice.1, bf16[768]{0:T(1024)(128)(2,1)S(1)} %dynamic-update-slice, ...), channel_id=1, replica_groups=mesh['rep'=8,'shard'=4] {'shard'}, use_global_device_ids=true, to_apply=%add.5 | all-reduce | flops 3072 | bytes 12288
  30.4 14.9 %all_gather.89 = bf16[768,128]{1,0:T(8,128)(2,1)S(1)} all-gather(bf16[192,128]{1,0:T(8,128)(2,1)S(1)} %copy-done.179), channel_id=1, replica_groups=mesh['rep'=8,'shard'=4] {'shard'}, dimensions={0}, use_global_device_ids=true | all-gather | bytes 245760 | tf_op jit(solution)/shard_map/all_gather | solution.py:154
  51.4 34.1 %all-gather.17.cloned.1.call-done = bf16[768,2304]{1,0:T(8,128)(2,1)} async-done(((bf16[192,2304]{1,0:T(8,128)(2,1)}), bf16[768,2304]{1,0:T(8,128)(2,1)}) %all-gather.17.cloned.1.call-update) | async-done | bytes 3538960 | tf_op jit(solution)/shard_map/all_gather | solution.py:153
  159.9 30.2 %all-gather.2 = bf16[48,128,64]{1,2,0:T(8,128)(2,1)} all-gather(bf16[12,128,64]{1,2,0:T(8,128)(2,1)S(1)} %convolution_convert_fusion.6), channel_id=4, replica_groups=mesh['rep'=8,'shard'=4] {'shard'}, dimensions={0}, use_global_device_ids=true | all-gather | bytes 983040 | tf_op jit(solution)/shard_map/all_gather | solution.py:18
  190.1 13.3 %all-gather.9 = bf16[4,12,128]{2,1,0:T(8,128)(2,1)S(1)} all-gather(bf16[1,12,128]{2,1,0:T(8,128)(2,1)S(1)} %bitcast.581), channel_id=5, replica_groups=mesh['rep'=8,'shard'=4] {'shard'}, dimensions={0}, use_global_device_ids=true | all-gather | bytes 15360 | tf_op jit(solution)/shard_map/all_gather | solution.py:18
  203.4 6.6 while.63
  226.2 4.9 fusion.40
  249.9 30.3 %all-gather = bf16[48,128,64]{1,2,0:T(8,128)(2,1)} all-gather(bf16[12,128,64]{1,2,0:T(8,128)(2,1)S(1)} %convolution_convert_fusion.7), channel_id=2, replica_groups=mesh['rep'=8,'shard'=4] {'shard'}, dimensions={0}, use_global_device_ids=true | all-gather | bytes 983040 | tf_op jit(solution)/shard_map/all_gather | solution.py:18
  280.2 13.9 %all-gather.8 = bf16[4,12,128]{2,1,0:T(8,128)(2,1)S(1)} all-gather(bf16[1,12,128]{2,1,0:T(8,128)(2,1)S(1)} %bitcast.580), channel_id=3, replica_groups=mesh['rep'=8,'shard'=4] {'shard'}, dimensions={0}, use_global_device_ids=true | all-gather | bytes 15360 | tf_op jit(solution)/shard_map/all_gather | solution.py:18
  294.1 6.6 while.62
  332.0 5.6 fusion.215
  340.8 6.4 fusion.21
  400.3 19.6 %all-gather.6 = bf16[48,128,64]{1,2,0:T(8,128)(2,1)} all-gather(bf16[12,128,64]{1,2,0:T(8,128)(2,1)S(1)} %copy-done.148), channel_id=8, replica_groups=mesh['rep'=8,'shard'=4] {'shard'}, dimensions={0}, use_global_device_ids=true | all-gather | bytes 983040 | tf_op jit(solution)/shard_map/all_gather | solution.py:43
  419.9 13.1 %all-gather.11 = bf16[4,12,128]{2,1,0:T(8,128)(2,1)S(1)} all-gather(bf16[1,12,128]{2,1,0:T(8,128)(2,1)S(1)} %bitcast.583), channel_id=9, replica_groups=mesh['rep'=8,'shard'=4] {'shard'}, dimensions={0}, use_global_device_ids=true | all-gather | bytes 15360 | tf_op jit(solution)/shard_map/all_gather | solution.py:43
  474.4 16.5 %all-gather.4 = bf16[48,128,64]{1,2,0:T(8,128)(2,1)} all-gather(bf16[12,128,64]{1,2,0:T(8,128)(2,1)S(1)} %copy-done.147), channel_id=6, replica_groups=mesh['rep'=8,'shard'=4] {'shard'}, dimensions={0}, use_global_device_ids=true | all-gather | bytes 983040 | tf_op jit(solution)/shard_map/all_gather | solution.py:43
  490.9 13.1 %all-gather.10 = bf16[4,12,128]{2,1,0:T(8,128)(2,1)S(1)} all-gather(bf16[1,12,128]{2,1,0:T(8,128)(2,1)S(1)} %bitcast.582), channel_id=7, replica_groups=mesh['rep'=8,'shard'=4] {'shard'}, dimensions={0}, use_global_device_ids=true | all-gather | bytes 15360 | tf_op jit(solution)/shard_map/all_gather | solution.py:43
  599.4 5.2 fusion.78
  604.8 24.6 %reduce-scatter.6.cloned.1.call-done = bf16[192,2304]{1,0:T(8,128)(2,1)} async-done(((bf16[768,2304]{1,0:T(8,128)(2,1)}), bf16[192,2304]{1,0:T(8,128)(2,1)}) %reduce-scatter.6.cloned.1.call-update) | async-done | bytes 884752 | tf_op jit(solution)/shard_map/reduce_scatter | solution.py:299
  629.4 87.9 %reduce-scatter.12.cloned.1.call-done = bf16[192,3072]{1,0:T(8,128)(2,1)} async-done(((bf16[768,3072]{1,0:T(8,128)(2,1)}), bf16[192,3072]{1,0:T(8,128)(2,1)}) %reduce-scatter.12.cloned.1.call-update) | async-done | bytes 1179664 | tf_op jit(solution)/shard_map/reduce_scatter | solution.py:314
  717.2 88.1 %reduce-scatter.14.cloned.1.call-done = bf16[768,768]{1,0:T(8,128)(2,1)} async-done(((bf16[3072,768]{1,0:T(8,128)(2,1)}), bf16[768,768]{1,0:T(8,128)(2,1)}) %reduce-scatter.14.cloned.1.call-update) | async-done | bytes 1179664 | tf_op jit(solution)/shard_map/reduce_scatter | solution.py:317
  806.0 11.1 %all-reduce.14 = (bf16[768]{0:T(1024)(128)(2,1)S(1)}, bf16[768]{0:T(1024)(128)(2,1)S(1)}, bf16[768]{0:T(1024)(128)(2,1)S(1)}, bf16[768]{0:T(1024)(128)(2,1)S(1)}) all-reduce(bf16[768]{0:T(1024)(128)(2,1)S(1)} %copy-done.224, bf16[768]{0:T(1024)(128)(2,1)S(1)} %add_convert_fusion.14, ...), channel_id=10, replica_groups=mesh['rep'=8,'shard'=4] {'shard'}, use_global_device_ids=true, to_apply=%region_70.71.clone | all-reduce | flops 3072 | bytes 12288
  817.4 5.4 fusion.79
  828.2 24.5 %all-reduce.12 = (bf16[192]{0:T(256)(128)(2,1)S(1)}, bf16[192]{0:T(256)(128)(2,1)S(1)}, bf16[192,128]{1,0:T(8,128)(2,1)S(1)}, bf16[192]{0:T(256)(128)(2,1)S(1)}, bf16[192]{0:T(256)(128)(2,1)S(1)}) all-reduce(bf16[192]{0:T(256)(128)(2,1)S(1)} %dynamic-slice.5, ...), channel_id=1, replica_groups=mesh['rep'=8,'shard'=4] {'rep'}, use_global_device_ids=true, to_apply=%region_71.72 | all-reduce | flops 25344 | bytes 101376 | tf_op jit(solution)/shard_map/psum | solution.py:322
  855.6 49.7 %all-reduce.18.cloned.1.call-done = (bf16[192,2304]{1,0:T(8,128)(2,1)}, bf16[192,768]{1,0:T(8,128)(2,1)}, bf16[192,3072]{1,0:T(8,128)(2,1)}, bf16[768,768]{1,0:T(8,128)(2,1)}) async-done(((bf16[192,2304]{1,0:T(8,128)(2,1)}, bf16[192,768]{1,0:T(8,128)(2,1)}, bf16[192,3072]{1,0:T(8,128)(2,1)}, bf16[768,768]{1,0:T(8,128)(2,1)}), (bf16[192,2304]{1,0:T(8,128)(2,1)}, bf16[192,768]{1,0:T(8,128)(2,1)}, ...) | async-done | bytes 3538960 | tf_op jit(solution)/shard_map/psum | solution.py:324
  (828 shorter events, 381.6 us)
Async XLA Ops:
  7.2 78.3 %all-gather.17.cloned.1.call-start = ((), (), s32[]{:S(2)}) async-start(), calls=%async_computation.5 | async-start | bytes 4423680 | tf_op jit(solution)/shard_map/all_gather | solution.py:153
  7.9 313.2 %all-gather.19.cloned.1.call-start = ((), (), s32[]{:S(2)}) async-start(), calls=%async_computation.6 | async-start | bytes 1474560 | tf_op jit(solution)/shard_map/all_gather | solution.py:155
  8.7 323.3 %all-gather.21.cloned.1.call-start = ((), (), s32[]{:S(2)}) async-start(), calls=%async_computation.7 | async-start | bytes 5898240 | tf_op jit(solution)/shard_map/all_gather | solution.py:158
  9.5 20.9 %copy-start.179 = (bf16[192,128]{1,0:T(8,128)(2,1)S(1)}, bf16[192,128]{1,0:T(8,128)(2,1)}, u32[]{:S(2)}) copy-start(bf16[192,128]{1,0:T(8,128)(2,1)} %param.23) | copy-start | bytes 147460
  9.5 331.4 %all-gather.23.cloned.1.call-start = ((), (), s32[]{:S(2)}) async-start(), calls=%async_computation.8 | async-start | bytes 5898240 | tf_op jit(solution)/shard_map/all_gather | solution.py:159
  10.0 594.7 %reduce-scatter.10.cloned.1.call-start = ((), (), s32[]{:S(2)}) async-start(), calls=%async_computation.11 | async-start | bytes 1474560 | tf_op jit(solution)/shard_map/reduce_scatter | solution.py:305
  10.9 34.4 %copy-start.180 = (f32[256]{0:T(256)}, f32[256]{0:T(256)S(1)}, u32[]{:S(2)}) copy-start(f32[256]{0:T(256)S(1)} %get-tuple-element.658) | copy-start | bytes 3076
  10.9 34.4 %copy-start.188 = (f32[256]{0:T(256)}, f32[256]{0:T(256)S(1)}, u32[]{:S(2)}) copy-start(f32[256]{0:T(256)S(1)} %get-tuple-element.657) | copy-start | bytes 3076
  11.8 33.5 %copy-start.215 = (f32[256]{0:T(256)}, f32[256]{0:T(256)S(1)}, u32[]{:S(2)}) copy-start(f32[256]{0:T(256)S(1)} %get-tuple-element.512) | copy-start | bytes 3076
  47.2 45.6 %copy-start.72 = (bf16[12,64,1,64]{1,3,0,2:T(8,128)(2,1)}, bf16[12,64,1,64]{1,3,0,2:T(8,128)(2,1)S(1)}, u32[]{:S(2)}) copy-start(bf16[12,64,1,64]{1,3,0,2:T(8,128)(2,1)S(1)} %copy.272) | copy-start | bytes 294916
  47.5 51.9 %copy-start.75 = (bf16[12,64,1,64]{1,3,0,2:T(8,128)(2,1)}, bf16[12,64,1,64]{1,3,0,2:T(8,128)(2,1)S(1)}, u32[]{:S(2)}) copy-start(bf16[12,64,1,64]{1,3,0,2:T(8,128)(2,1)S(1)} %copy.273) | copy-start | bytes 294916
  102.9 56.7 %copy-start.63 = (bf16[256,12,64]{0,2,1:T(8,128)(2,1)}, bf16[256,12,64]{0,2,1:T(8,128)(2,1)S(1)}, u32[]{:S(2)}) copy-start(bf16[256,12,64]{0,2,1:T(8,128)(2,1)S(1)} %divide_convert_fusion) | copy-start | bytes 1179652
  158.3 31.8 %copy-start.83 = (bf16[256,768]{0,1:T(8,128)(2,1)}, bf16[256,768]{0,1:T(8,128)(2,1)S(1)}, u32[]{:S(2)}) copy-start(bf16[256,768]{0,1:T(8,128)(2,1)S(1)} %copy.174) | copy-start | bytes 1179652
  159.5 30.6 %copy-start.199 = (bf16[12,128]{1,0:T(8,128)(2,1)S(1)}, bf16[12,128]{1,0:T(8,128)(2,1)}, u32[]{:S(2)}) copy-start(bf16[12,128]{1,0:T(8,128)(2,1)} %fusion.139) | copy-start | bytes 9220
  248.2 32.0 %copy-start.81 = (bf16[256,768]{0,1:T(8,128)(2,1)}, bf16[256,768]{0,1:T(8,128)(2,1)S(1)}, u32[]{:S(2)}) copy-start(bf16[256,768]{0,1:T(8,128)(2,1)S(1)} %copy.157) | copy-start | bytes 1179652
  249.5 30.7 %copy-start.198 = (bf16[12,128]{1,0:T(8,128)(2,1)S(1)}, bf16[12,128]{1,0:T(8,128)(2,1)}, u32[]{:S(2)}) copy-start(bf16[12,128]{1,0:T(8,128)(2,1)} %fusion.140) | copy-start | bytes 9220
  302.6 11.5 %copy-start.2 = (bf16[4,64,12,128]{3,1,2,0:T(8,128)(2,1)}, bf16[4,64,12,128]{3,1,2,0:T(8,128)(2,1)S(1)}, u32[]{:S(2)}) copy-start(bf16[4,64,12,128]{3,1,2,0:T(8,128)(2,1)S(1)} %get-tuple-element.589) | copy-start | bytes 2359300
  323.3 34.7 %copy-start.11 = (f32[256,768]{1,0:T(8,128)}, f32[256,768]{1,0:T(8,128)S(1)}, u32[]{:S(2)}) copy-start(f32[256,768]{1,0:T(8,128)S(1)} %get-tuple-element.636) | copy-start | bytes 2359300
  470.6 20.4 %copy-start.200 = (bf16[12,128]{1,0:T(8,128)(2,1)S(1)}, bf16[12,128]{1,0:T(8,128)(2,1)}, u32[]{:S(2)}) copy-start(bf16[12,128]{1,0:T(8,128)(2,1)} %fusion.187) | copy-start | bytes 9220
  536.8 92.5 %reduce-scatter.6.cloned.1.call-start = ((), (), s32[]{:S(2)}) async-start(), calls=%async_computation.9 | async-start | bytes 4423680 | tf_op jit(solution)/shard_map/reduce_scatter | solution.py:299
  566.5 150.8 %reduce-scatter.12.cloned.1.call-start = ((), (), s32[]{:S(2)}) async-start(), calls=%async_computation.12 | async-start | bytes 5898240 | tf_op jit(solution)/shard_map/reduce_scatter | solution.py:314
  574.7 230.6 %reduce-scatter.14.cloned.1.call-start = ((), (), s32[]{:S(2)}) async-start(), calls=%async_computation.13 | async-start | bytes 5898240 | tf_op jit(solution)/shard_map/reduce_scatter | solution.py:317
  584.0 244.1 %reduce-scatter.8.cloned.1.call-start = ((), (), s32[]{:S(2)}) async-start(), calls=%async_computation.10 | async-start | bytes 245760 | tf_op jit(solution)/shard_map/reduce_scatter | solution.py:302
  599.2 306.1 %all-reduce.18.cloned.1.call-start = ((), (), s32[]{:S(2)}) async-start(), calls=%async_computation.14 | async-start | bytes 7077888 | tf_op jit(solution)/shard_map/psum | solution.py:324
  (231 other events, 687.1 us)
Sparse Core Ops, SparseCore 0:
  9.6 75.8 all-gather.16
  87.1 29.1 all-gather.18
  117.9 101.2 all-gather.20
  220.5 100.6 all-gather.22
  536.9 25.0 reduce-scatter.9
  566.5 62.7 reduce-scatter.5
  631.7 85.5 reduce-scatter.11
  719.5 85.7 reduce-scatter.13
  808.2 19.9 reduce-scatter.7
  832.1 73.0 all-reduce.17
where the time goes:
time: 925 us; the launch traced here: 919 us
  waiting for transfers between devices  289 us (31%)
  blocking collectives  215 us (23%)
  matrix products  169 us (18%)
  local copies, waits for them, and re-layouts  144 us (16%)
  other arithmetic  81.6 us (9%)
  between operations  18.6 us (2%)
    reduce_scatter x1, waiting for transfers between devices, shards(): lax.psum_scatter(totals[8].astype(jnp.bfloat16), 'shard', scatter_dimensi...  88.1 us
    reduce_scatter x1, waiting for transfers between devices, shards(): lax.psum_scatter(totals[7].astype(jnp.bfloat16), 'shard', scatter_dimensi...  87.9 us
    all_gather x4, blocking collectives, prefix(): lax.all_gather(part.astype(kind), axis)  87.6 us
    all_gather x4, blocking collectives, prefix_2(): lax.all_gather(a.astype(kind), axis)  62.3 us
    psum x1, waiting for transfers between devices, shards(): lax.psum(shares[2].astype(jnp.bfloat16), 'rep').astype(jnp.float32)  49.7 us
    all_gather x1, waiting for transfers between devices, shards(): lax.all_gather(w_qkv, 'shard', axis=0, tiled=True)  34.1 us
    unnamed x505, local copies, waits for them, and re-layouts  32.8 us
    concatenate x16, local copies, waits for them, and re-layouts, featurize(): jnp.concatenate([jax.nn.softmax(inputs, axis=-1), jax.nn.softmax(-inputs,...  32.5 us
  transfers between devices with their start and end apart: 10, of which 6 were waited for; matrix products, arithmetic and copies ran while one was open for 27% of the time, Pallas kernels for 0%

commit v1 on v0

--- a/solution.py
+++ b/solution.py
@@ -321,7 +321,7 @@
     reduced = (
         lax.psum(shares[0].astype(jnp.bfloat16), "rep").astype(jnp.float32),
         lax.psum(shares[1].astype(jnp.bfloat16), "rep").astype(jnp.float32),
-        lax.psum(shares[2].astype(jnp.bfloat16), "rep").astype(jnp.float32),
+        jnp.sum(lax.all_gather(shares[2].astype(jnp.bfloat16), "rep"), axis=0).astype(jnp.float32),
         lax.psum(shares[3].astype(jnp.bfloat16), "rep").astype(jnp.float32),
         lax.psum(shares[4].astype(jnp.bfloat16), "rep").astype(jnp.float32),
         lax.psum(shares[5].astype(jnp.bfloat16), "rep").astype(jnp.float32),

time: 925 us -> 837 us (0.905)
  waiting for transfers between devices: 289 us -> 176 us
  blocking collectives: 215 us -> 237 us
  other arithmetic: 81.6 us -> 94.1 us
    reduce_scatter x1, waiting for transfers between devices: 88.1 us -> 0.02 us  [shards(): lax.psum_scatter(totals[8].astype(jnp.bfloat16), 'shard', scatter_dimensi...]
    reduce_scatter x1, waiting for transfers between devices: 87.9 us -> 0.02 us  [shards(): lax.psum_scatter(totals[7].astype(jnp.bfloat16), 'shard', scatter_dimensi...]
    all_gather x0 -> x1, waiting for transfers between devices: none -> 44 us  [shards(): lax.all_gather(shares[2].astype(jnp.bfloat16), 'rep')]
    reduce_scatter x1, waiting for transfers between devices: 24.6 us -> 63.9 us  [shards(): lax.psum_scatter(totals[2].astype(jnp.bfloat16), 'shard', scatter_dimensi...]
    all_gather x4, blocking collectives: 62.3 us -> 86.2 us  [prefix_2(): lax.all_gather(a.astype(kind), axis)]
    psum x1, waiting for transfers between devices: 49.7 us -> 32.2 us  [shards(): lax.psum(shares[4].astype(jnp.bfloat16), 'rep').astype(jnp.float32)]
    unnamed x505 -> x507, local copies, waits for them, and re-layouts: 32.8 us -> 35.8 us
  transfers between devices with their start and end apart: 10 -> 11, of which waited for: 6 -> 4; matrix products, arithmetic and copies ran while one was open for 27% -> 41% of each run, Pallas kernels for 0% -> 0%
where the time goes in v1:
time: 837 us; the launch traced here: 831 us
  blocking collectives  237 us (28%)
  waiting for transfers between devices  176 us (21%)
  matrix products  161 us (19%)
  local copies, waits for them, and re-layouts  142 us (17%)
  other arithmetic  94.1 us (11%)
  between operations  18.4 us (2%)
    all_gather x4, blocking collectives, prefix(): lax.all_gather(part.astype(kind), axis)  86.6 us
    all_gather x4, blocking collectives, prefix_2(): lax.all_gather(a.astype(kind), axis)  86.2 us
    reduce_scatter x1, waiting for transfers between devices, shards(): lax.psum_scatter(totals[2].astype(jnp.bfloat16), 'shard', scatter_dimensi...  63.9 us
    all_gather x1, waiting for transfers between devices, shards(): lax.all_gather(shares[2].astype(jnp.bfloat16), 'rep')  44 us
    unnamed x507, local copies, waits for them, and re-layouts  35.8 us
    all_gather x1, waiting for transfers between devices, shards(): lax.all_gather(w_qkv, 'shard', axis=0, tiled=True)  32.9 us
    concatenate x16, local copies, waits for them, and re-layouts, featurize(): jnp.concatenate([jax.nn.softmax(inputs, axis=-1), jax.nn.softmax(-inputs,...  32.6 us
    psum x1, waiting for transfers between devices, shards(): lax.psum(shares[4].astype(jnp.bfloat16), 'rep').astype(jnp.float32)  32.2 us
  transfers between devices with their start and end apart: 11, of which 4 were waited for; matrix products, arithmetic and copies ran while one was open for 41% of the time, Pallas kernels for 0%

profile of v1, /device:TPU:0, one launch (start us, length us, event | category | flops | bytes accessed | tf_op | source)
XLA Modules:
  0.0 830.8 jit_solution(15256209220822570480)
XLA Ops:
  14.7 14.5 %all-reduce.15 = (bf16[768]{0:T(1024)(128)(2,1)S(1)}, bf16[768]{0:T(1024)(128)(2,1)S(1)}, bf16[768]{0:T(1024)(128)(2,1)}, bf16[768]{0:T(1024)(128)(2,1)}) all-reduce(bf16[768]{0:T(1024)(128)(2,1)S(1)} %dynamic-update-slice.1, bf16[768]{0:T(1024)(128)(2,1)S(1)} %dynamic-update-slice, ...), channel_id=1, replica_groups=mesh['rep'=8,'shard'=4] {'shard'}, use_global_device_ids=true, to_apply=%add.5 | all-reduce | flops 3072 | bytes 12288
  30.4 14.9 %all_gather.95 = bf16[768,128]{1,0:T(8,128)(2,1)S(1)} all-gather(bf16[192,128]{1,0:T(8,128)(2,1)S(1)} %copy-done.190), channel_id=1, replica_groups=mesh['rep'=8,'shard'=4] {'shard'}, dimensions={0}, use_global_device_ids=true | all-gather | bytes 245760 | tf_op jit(solution)/shard_map/all_gather | solution.py:154
  52.6 32.9 %all-gather.19.cloned.1.call-done = bf16[768,2304]{1,0:T(8,128)(2,1)} async-done(((bf16[192,2304]{1,0:T(8,128)(2,1)}), bf16[768,2304]{1,0:T(8,128)(2,1)}) %all-gather.19.cloned.1.call-update) | async-done | bytes 3538960 | tf_op jit(solution)/shard_map/all_gather | solution.py:153
  165.1 30.2 %all-gather.2 = bf16[48,128,64]{1,2,0:T(8,128)(2,1)} all-gather(bf16[12,128,64]{1,2,0:T(8,128)(2,1)S(1)} %convolution_convert_fusion.6), channel_id=4, replica_groups=mesh['rep'=8,'shard'=4] {'shard'}, dimensions={0}, use_global_device_ids=true | all-gather | bytes 983040 | tf_op jit(solution)/shard_map/all_gather | solution.py:18
  195.3 13.4 %all-gather.10 = bf16[4,12,128]{2,1,0:T(8,128)(2,1)S(1)} all-gather(bf16[1,12,128]{2,1,0:T(8,128)(2,1)S(1)} %bitcast.583), channel_id=5, replica_groups=mesh['rep'=8,'shard'=4] {'shard'}, dimensions={0}, use_global_device_ids=true | all-gather | bytes 15360 | tf_op jit(solution)/shard_map/all_gather | solution.py:18
  208.7 6.6 while.63
  254.8 29.7 %all-gather = bf16[48,128,64]{1,2,0:T(8,128)(2,1)} all-gather(bf16[12,128,64]{1,2,0:T(8,128)(2,1)S(1)} %convolution_convert_fusion.7), channel_id=2, replica_groups=mesh['rep'=8,'shard'=4] {'shard'}, dimensions={0}, use_global_device_ids=true | all-gather | bytes 983040 | tf_op jit(solution)/shard_map/all_gather | solution.py:18
  284.5 13.3 %all-gather.9 = bf16[4,12,128]{2,1,0:T(8,128)(2,1)S(1)} all-gather(bf16[1,12,128]{2,1,0:T(8,128)(2,1)S(1)} %bitcast.582), channel_id=3, replica_groups=mesh['rep'=8,'shard'=4] {'shard'}, dimensions={0}, use_global_device_ids=true | all-gather | bytes 15360 | tf_op jit(solution)/shard_map/all_gather | solution.py:18
  297.8 6.6 while.62
  336.7 5.7 fusion.215
  345.6 6.6 fusion.21
  369.7 4.6 fusion.255
  402.0 4.6 fusion.29
  424.7 14.0 %all-gather.12 = bf16[4,12,128]{2,1,0:T(8,128)(2,1)} all-gather(bf16[1,12,128]{2,1,0:T(8,128)(2,1)S(1)} %bitcast.584), channel_id=9, replica_groups=mesh['rep'=8,'shard'=4] {'shard'}, dimensions={0}, use_global_device_ids=true | all-gather | bytes 15360 | tf_op jit(solution)/shard_map/all_gather | solution.py:43
  440.0 30.0 %all-gather.6 = bf16[48,128,64]{1,2,0:T(8,128)(2,1)} all-gather(bf16[12,128,64]{1,2,0:T(8,128)(2,1)S(1)} %copy-done.150), channel_id=8, replica_groups=mesh['rep'=8,'shard'=4] {'shard'}, dimensions={0}, use_global_device_ids=true | all-gather | bytes 983040 | tf_op jit(solution)/shard_map/all_gather | solution.py:43
  492.0 6.6 while.61
  525.8 13.3 %all-gather.11 = bf16[4,12,128]{2,1,0:T(8,128)(2,1)S(1)} all-gather(bf16[1,12,128]{2,1,0:T(8,128)(2,1)S(1)} %bitcast.585), channel_id=7, replica_groups=mesh['rep'=8,'shard'=4] {'shard'}, dimensions={0}, use_global_device_ids=true | all-gather | bytes 15360 | tf_op jit(solution)/shard_map/all_gather | solution.py:43
  539.1 28.9 %all-gather.4 = bf16[48,128,64]{1,2,0:T(8,128)(2,1)} all-gather(bf16[12,128,64]{1,2,0:T(8,128)(2,1)} %get-tuple-element.651), channel_id=6, replica_groups=mesh['rep'=8,'shard'=4] {'shard'}, dimensions={0}, use_global_device_ids=true | all-gather | bytes 983040 | tf_op jit(solution)/shard_map/all_gather | solution.py:43
  613.6 63.9 %reduce-scatter.6.cloned.1.call-done = bf16[192,2304]{1,0:T(8,128)(2,1)} async-done(((bf16[768,2304]{1,0:T(8,128)(2,1)}), bf16[192,2304]{1,0:T(8,128)(2,1)}) %reduce-scatter.6.cloned.1.call-update) | async-done | bytes 884752 | tf_op jit(solution)/shard_map/reduce_scatter | solution.py:299
  684.0 10.9 %all-reduce.14 = (bf16[768]{0:T(1024)(128)(2,1)S(1)}, bf16[768]{0:T(1024)(128)(2,1)S(1)}, bf16[768]{0:T(1024)(128)(2,1)S(1)}, bf16[768]{0:T(1024)(128)(2,1)S(1)}) all-reduce(bf16[768]{0:T(1024)(128)(2,1)S(1)} %add_convert_fusion.15, bf16[768]{0:T(1024)(128)(2,1)S(1)} %add_convert_fusion.14, ...), channel_id=11, replica_groups=mesh['rep'=8,'shard'=4] {'shard'}, use_global_device_ids=true, to_apply=%region_70.71.clone | all-reduce | flops 3072 | bytes 12288
  695.3 5.4 fusion.78
  708.4 24.2 %all-reduce.12 = (bf16[192]{0:T(256)(128)(2,1)S(1)}, bf16[192]{0:T(256)(128)(2,1)S(1)}, bf16[192,128]{1,0:T(8,128)(2,1)S(1)}, bf16[192]{0:T(256)(128)(2,1)S(1)}, bf16[192]{0:T(256)(128)(2,1)S(1)}) all-reduce(bf16[192]{0:T(256)(128)(2,1)S(1)} %dynamic-slice.5, ...), channel_id=1, replica_groups=mesh['rep'=8,'shard'=4] {'rep'}, use_global_device_ids=true, to_apply=%region_71.72 | all-reduce | flops 25344 | bytes 101376 | tf_op jit(solution)/shard_map/psum | solution.py:322
  735.6 32.2 %all-reduce.18.cloned.1.call-done = (bf16[192,768]{1,0:T(8,128)(2,1)}, bf16[192,3072]{1,0:T(8,128)(2,1)}, bf16[768,768]{1,0:T(8,128)(2,1)}) async-done(((bf16[192,768]{1,0:T(8,128)(2,1)}, bf16[192,3072]{1,0:T(8,128)(2,1)}, bf16[768,768]{1,0:T(8,128)(2,1)}), (bf16[192,768]{1,0:T(8,128)(2,1)}, bf16[192,3072]{1,0:T(8,128)(2,1)}, bf16[768,768]{1,0:T(8,128)(2,1)})) %all-reduce.18.cloned.1.call-update) | async-done | bytes 2654224 | tf_op jit(solution)/shard_map/psum | solution.py:326
  774.2 44.0 %all-gather.27.cloned.1.call-done = bf16[1536,2304]{1,0:T(8,128)(2,1)} async-done(((bf16[192,2304]{1,0:T(8,128)(2,1)}), bf16[1536,2304]{1,0:T(8,128)(2,1)}) %all-gather.27.cloned.1.call-update) | async-done | bytes 7077904 | tf_op jit(solution)/shard_map/all_gather | solution.py:324
  (833 shorter events, 378.3 us)
Async XLA Ops:
  7.2 78.3 %all-gather.19.cloned.1.call-start = ((), (), s32[]{:S(2)}) async-start(), calls=%async_computation.5 | async-start | bytes 4423680 | tf_op jit(solution)/shard_map/all_gather | solution.py:153
  7.9 317.9 %all-gather.21.cloned.1.call-start = ((), (), s32[]{:S(2)}) async-start(), calls=%async_computation.6 | async-start | bytes 1474560 | tf_op jit(solution)/shard_map/all_gather | solution.py:155
  8.7 328.0 %all-gather.23.cloned.1.call-start = ((), (), s32[]{:S(2)}) async-start(), calls=%async_computation.7 | async-start | bytes 5898240 | tf_op jit(solution)/shard_map/all_gather | solution.py:158
  9.5 336.1 %all-gather.25.cloned.1.call-start = ((), (), s32[]{:S(2)}) async-start(), calls=%async_computation.8 | async-start | bytes 5898240 | tf_op jit(solution)/shard_map/all_gather | solution.py:159
  10.0 602.9 %reduce-scatter.10.cloned.1.call-start = ((), (), s32[]{:S(2)}) async-start(), calls=%async_computation.11 | async-start | bytes 1474560 | tf_op jit(solution)/shard_map/reduce_scatter | solution.py:305
  10.9 34.4 %copy-start.191 = (f32[256]{0:T(256)}, f32[256]{0:T(256)S(1)}, u32[]{:S(2)}) copy-start(f32[256]{0:T(256)S(1)} %get-tuple-element.657) | copy-start | bytes 3076
  48.4 44.0 %copy-start.85 = (bf16[12,64,1,64]{1,3,0,2:T(8,128)(2,1)}, bf16[12,64,1,64]{1,3,0,2:T(8,128)(2,1)S(1)}, u32[]{:S(2)}) copy-start(bf16[12,64,1,64]{1,3,0,2:T(8,128)(2,1)S(1)} %copy.272) | copy-start | bytes 294916
  48.8 50.7 %copy-start.87 = (bf16[12,64,1,64]{1,3,0,2:T(8,128)(2,1)}, bf16[12,64,1,64]{1,3,0,2:T(8,128)(2,1)S(1)}, u32[]{:S(2)}) copy-start(bf16[12,64,1,64]{1,3,0,2:T(8,128)(2,1)S(1)} %copy.273) | copy-start | bytes 294916
  94.4 54.4 %copy-start.15 = (f32[256,12,64]{0,2,1:T(8,128)}, f32[256,12,64]{0,2,1:T(8,128)S(1)}, u32[]{:S(2)}) copy-start(f32[256,12,64]{0,2,1:T(8,128)S(1)} %get-tuple-element.625) | copy-start | bytes 2359300
  103.5 61.2 %copy-start.75 = (bf16[256,12,64]{0,2,1:T(8,128)(2,1)}, bf16[256,12,64]{0,2,1:T(8,128)(2,1)S(1)}, u32[]{:S(2)}) copy-start(bf16[256,12,64]{0,2,1:T(8,128)(2,1)S(1)} %divide_convert_fusion) | copy-start | bytes 1179652
  306.4 168.1 %copy-start.1 = (bf16[4,64,12,128]{3,1,2,0:T(8,128)(2,1)}, bf16[4,64,12,128]{3,1,2,0:T(8,128)(2,1)S(1)}, u32[]{:S(2)}) copy-start(bf16[4,64,12,128]{3,1,2,0:T(8,128)(2,1)S(1)} %get-tuple-element.588) | copy-start | bytes 2359300
  327.9 61.7 %copy-start.13 = (f32[256,768]{1,0:T(8,128)}, f32[256,768]{1,0:T(8,128)S(1)}, u32[]{:S(2)}) copy-start(f32[256,768]{1,0:T(8,128)S(1)} %get-tuple-element.635) | copy-start | bytes 2359300
  379.5 233.6 %reduce-scatter.12.cloned.1.call-start = ((), (), s32[]{:S(2)}) async-start(), calls=%async_computation.12 | async-start | bytes 5898240 | tf_op jit(solution)/shard_map/reduce_scatter | solution.py:314
  393.5 219.6 %reduce-scatter.14.cloned.1.call-start = ((), (), s32[]{:S(2)}) async-start(), calls=%async_computation.13 | async-start | bytes 5898240 | tf_op jit(solution)/shard_map/reduce_scatter | solution.py:317
  423.9 52.0 %copy-start.163 = (f32[4,12,64]{2,1,0:T(8,128)}, f32[4,12,64]{2,1,0:T(8,128)S(1)}, u32[]{:S(2)}) copy-start(f32[4,12,64]{2,1,0:T(8,128)S(1)} %get-tuple-element.613) | copy-start | bytes 36868
  424.6 45.4 %copy-start.62 = (f32[4,64,12,64]{1,0,3,2:T(4,128)S(1)}, f32[4,64,12,64]{1,0,3,2:T(4,128)}, u32[]{:S(2)}) copy-start(f32[4,64,12,64]{1,0,3,2:T(4,128)} %reshape_reshape.6) | copy-start | bytes 2359300
  424.6 45.4 %copy-start.194 = (f32[4,64,12]{1,2,0:T(8,128)S(1)}, f32[4,64,12]{1,2,0:T(8,128)}, u32[]{:S(2)}) copy-start(f32[4,64,12]{1,2,0:T(8,128)} %copy-done.193) | copy-start | bytes 36868
  498.6 178.9 %reduce-scatter.6.cloned.1.call-start = ((), (), s32[]{:S(2)}) async-start(), calls=%async_computation.9 | async-start | bytes 4423680 | tf_op jit(solution)/shard_map/reduce_scatter | solution.py:299
  608.5 99.9 %reduce-scatter.8.cloned.1.call-start = ((), (), s32[]{:S(2)}) async-start(), calls=%async_computation.10 | async-start | bytes 245760 | tf_op jit(solution)/shard_map/reduce_scatter | solution.py:302
  612.9 154.9 %all-reduce.18.cloned.1.call-start = ((), (), s32[]{:S(2)}) async-start(), calls=%async_computation.15 | async-start | bytes 5308416 | tf_op jit(solution)/shard_map/psum | solution.py:326
  613.0 65.2 %copy-start.116 = (bf16[12,256,64]{1,2,0:T(8,128)(2,1)S(1)}, bf16[12,256,64]{1,2,0:T(8,128)(2,1)}, u32[]{:S(2)}) copy-start(bf16[12,256,64]{1,2,0:T(8,128)(2,1)} %copy-done.115) | copy-start | bytes 1179652
  613.1 65.2 %copy-start.118 = (bf16[12,256,64]{1,2,0:T(8,128)(2,1)S(1)}, bf16[12,256,64]{1,2,0:T(8,128)(2,1)}, u32[]{:S(2)}) copy-start(bf16[12,256,64]{1,2,0:T(8,128)(2,1)} %copy-done.117) | copy-start | bytes 1179652
  613.1 65.2 %copy-start.120 = (bf16[256,12,64]{0,2,1:T(8,128)(2,1)S(1)}, bf16[256,12,64]{0,2,1:T(8,128)(2,1)}, u32[]{:S(2)}) copy-start(bf16[256,12,64]{0,2,1:T(8,128)(2,1)} %copy-done.119) | copy-start | bytes 1179652
  613.5 204.8 %all-gather.27.cloned.1.call-start = ((), (), s32[]{:S(2)}) async-start(), calls=%async_computation.14 | async-start | bytes 7962624 | tf_op jit(solution)/shard_map/all_gather | solution.py:324
  (232 other events, 928.3 us)
Sparse Core Ops, SparseCore 0:
  9.6 75.8 all-gather.18
  87.1 29.1 all-gather.20
  117.8 101.2 all-gather.22
  220.5 100.6 all-gather.24
  379.6 28.8 reduce-scatter.9
  410.6 96.8 reduce-scatter.11
  509.9 98.5 reduce-scatter.13
  610.8 66.6 reduce-scatter.5
  679.7 19.6 reduce-scatter.7
  703.3 64.4 all-reduce.17
  769.7 48.5 all-gather.26
